TPU v7x, 512 devices: a whole 4x8x8 slice. The times are simulated.
512 devices in a mesh: seq: 32 (over x, y), head: 16 (over z, core).
Axes of the slice: x: 4, y: 8, z: 8, core: 2. Of those that a mesh axis runs over, the one named last changes fastest.
Arguments:
- projected: bfloat16 [3, 4096, 2048], P(None, 'seq', 'head'), may hold values from -6 to 6
- out_grad: bfloat16 [4096, 2048], P('seq', 'head'), may hold values from -6 to 6
- logits: float32 [2, 16, 4096], P(None, 'head', 'seq'), may hold values from -6 to 6
- head_params: float32 [2, 16], P(None, 'head'), may hold values from -12 to 1, as said below
- qkv_weight: bfloat16 [3, 2048, 2048], P(None, None, 'head'), may hold values from -0.1875 to 0.1875
- gate_weight: bfloat16 [2, 16, 2048], P(None, 'head'), may hold values from -1.5 to 1.5
Outputs:
- input_grad: bfloat16 [4096, 2048], P('seq', 'head')
Inputs may be any that keep to these rules, and one draw needn't show every extreme that they name: `head_params`: row 0 holds the logarithms of the heads' decay scales, row 1 the decay biases.
All inputs are finite; a program needn't handle non-finite values.
Results may differ from a plain program's by a relative error of at most 0.0034.
Values sent between devices are 32-bit elements; how exact they have to be, the bound alone decides.
A program may use at most 64 MiB of HBM per device.

v0:
```python
import jax
import jax.numpy as jnp
from jax import lax
from jax.sharding import Mesh
from jax.sharding import PartitionSpec as P

DK = 128
BLOCK = 64
SEQ = ("seq_0", "seq_1")


exact_precision = lax.Precision.HIGHEST


def filled_with(x, identity):
    return jax.tree.map(
        lambda a, e: jnp.broadcast_to(jnp.asarray(e, a.dtype), a.shape), x, identity
    )


def carried_in(x, axes, combine, identity, reverse):
    before = start = filled_with(x, identity)
    running = x
    for axis in reversed(axes):
        peers, here = (lax.axis_size(axis), lax.axis_index(axis))
        pieces = jax.tree.map(lambda part: lax.all_gather(part, axis), running)
        inside, running = (start, start)
        for k in reversed(range(peers)) if reverse else range(peers):
            passed = k > here if reverse else k < here
            running = combine(running, jax.tree.map(lambda part: part[k], pieces))
            inside = jax.tree.map(lambda new, old: jnp.where(passed, new, old), running, inside)
        before = combine(inside, before)
    return before


def cut_along(x, dim, peers):
    shape = x.shape
    pieces = x.reshape(*shape[:dim], peers, shape[dim] // peers, *shape[dim + 1 :])
    return jnp.moveaxis(pieces, dim, 0)


def summed_on_arrival(x, axis, dim):
    pieces = cut_along(x, dim, lax.axis_size(axis))
    arrived = lax.all_to_all(pieces, axis, split_axis=0, concat_axis=0, tiled=True)
    return arrived.sum(axis=0)


def matmul(left, right):
    return jnp.matmul(left, right, precision=exact_precision)


def flip_last(array):
    return jnp.swapaxes(array, -1, -2)


def unit_rows(raw_rows):
    return raw_rows * lax.rsqrt(jnp.sum(raw_rows * raw_rows, axis=-1, keepdims=True) + 1.0)


def to_blocks(array, block_len):
    tok_rows, head_count, depth = array.shape
    return array.reshape(tok_rows // block_len, block_len, head_count, depth).transpose(0, 2, 1, 3)


def prepare(query_raw, key_raw, values, logit_rows, head_params, block_len):
    queries = to_blocks(unit_rows(query_raw) * DK ** (-0.5), block_len)
    keys = to_blocks(unit_rows(key_raw), block_len)
    value_rows = to_blocks(values, block_len)
    decay = -jnp.exp(head_params[0])[:, None] * jax.nn.softplus(
        logit_rows[0] + head_params[1][:, None]
    )
    head_count, tok_rows = decay.shape
    block_count = tok_rows // block_len
    cumul = jnp.cumsum(
        decay.reshape(head_count, block_count, block_len).transpose(1, 0, 2), axis=-1
    )
    write_gate = (
        jax.nn.sigmoid(logit_rows[1]).reshape(head_count, block_count, block_len).transpose(1, 0, 2)
    )
    row_index = lax.broadcasted_iota(jnp.int32, (block_len, block_len), 0)
    col_index = lax.broadcasted_iota(jnp.int32, (block_len, block_len), 1)
    lower_mask = row_index >= col_index
    strict_mask = row_index > col_index
    spread = cumul[..., :, None] - cumul[..., None, :]
    decay_ratio = jnp.where(lower_mask, jnp.exp(jnp.where(lower_mask, spread, 0.0)), 0.0)
    key_inner = matmul(keys, flip_last(keys))
    lower_part = jnp.where(strict_mask, decay_ratio * key_inner * write_gate[..., :, None], 0.0)
    inverse = jnp.eye(block_len, dtype=jnp.float32) - lower_part
    decay_power_matrix = lower_part
    reach_len = 2
    while reach_len < block_len:
        decay_power_matrix = matmul(decay_power_matrix, decay_power_matrix)
        inverse = inverse + matmul(inverse, decay_power_matrix)
        reach_len = reach_len * 2
    decayed = jnp.exp(cumul)
    base_values = matmul(inverse, write_gate[..., None] * value_rows)
    key_weights = matmul(inverse, (write_gate * decayed)[..., None] * keys)
    attend = decay_ratio * matmul(queries, flip_last(keys))
    query_decayed = decayed[..., None] * queries
    key_decayed = jnp.exp(cumul[..., -1:] - cumul)[..., None] * keys
    return (base_values, key_weights, attend, query_decayed, key_decayed, decayed[..., -1])


def block_run(pieces, start_state):

    def block_step(running_state, block_piece):
        base_values, key_weights, attend, query_decayed, key_decayed, last_decay = block_piece
        fresh_values = base_values - matmul(key_weights, running_state)
        out_rows = matmul(query_decayed, running_state) + matmul(attend, fresh_values)
        running_state = last_decay[:, None, None] * running_state + matmul(
            flip_last(key_decayed), fresh_values
        )
        return (running_state, out_rows)

    final_state, out_rows = lax.scan(block_step, start_state, pieces)
    return (out_rows, final_state)


def transition(pieces, eye_state):
    base_values, key_weights, attend, query_decayed, key_decayed, last_decay = pieces
    block_maps = last_decay[..., None, None] * eye_state - matmul(
        flip_last(key_decayed), key_weights
    )
    block_start_positions = matmul(flip_last(key_decayed), base_values)

    def transition_step(carry_pair, block_pair):
        step_matrix, offset = carry_pair
        block_map, block_offset = block_pair
        return ((matmul(block_map, step_matrix), matmul(block_map, offset) + block_offset), None)

    start_pair = (eye_state, jnp.zeros_like(eye_state))
    final_pair, unused = lax.scan(transition_step, start_pair, (block_maps, block_start_positions))
    return final_pair


def compose(earlier, later):
    return (matmul(later[0], earlier[0]), matmul(later[0], earlier[1]) + later[1])


def shards(projected, out_grad, logits, head_params, qkv_weight, gate_weight):
    tok_rows = projected.shape[1]
    head_count = projected.shape[2] // DK
    raw_inputs = projected.astype(jnp.float32).reshape(3, tok_rows, head_count, DK)
    out_blocks = to_blocks(out_grad.astype(jnp.float32).reshape(tok_rows, head_count, DK), BLOCK)

    def prep_fn(query_raw, key_raw, values, logit_rows):
        return prepare(query_raw, key_raw, values, logit_rows, head_params, BLOCK)

    pieces, pull_prepare = jax.vjp(prep_fn, raw_inputs[0], raw_inputs[1], raw_inputs[2], logits)
    eye_state = jnp.broadcast_to(jnp.eye(DK, dtype=jnp.float32), (head_count, DK, DK))
    zero_state = jnp.zeros((head_count, DK, DK), jnp.float32)
    step_matrix, offset = transition(pieces, eye_state)

    def state_only(start_state):
        return block_run(pieces, start_state)

    unused_out, pull_state = jax.vjp(state_only, zero_state)
    free_grad = pull_state((out_blocks, zero_state))[0]
    state_in = carried_in((step_matrix, offset), SEQ, compose, (eye_state, zero_state), False)[1]
    grad_out = carried_in(
        (flip_last(step_matrix), free_grad), SEQ, compose, (eye_state, zero_state), True
    )[1]
    unused_run, pull_run = jax.vjp(block_run, pieces, state_in)
    piece_grads, unused_grad = pull_run((out_blocks, grad_out))
    query_grad, key_grad, value_grad, logit_grad = pull_prepare(piece_grads)
    stacked_gradient = (
        jnp.stack([query_grad, key_grad, value_grad])
        .reshape(3, tok_rows, head_count * DK)
        .astype(jnp.bfloat16)
    )
    partial_term = jnp.einsum(
        "jtk,jdk->td", stacked_gradient, qkv_weight, preferred_element_type=jnp.float32
    )
    partial_term = partial_term + jnp.einsum(
        "jht,jhd->td", logit_grad, gate_weight.astype(jnp.float32), precision=exact_precision
    )
    return summed_on_arrival(partial_term, "head", 1).astype(jnp.bfloat16)


def solution(mesh):
    split = Mesh(mesh.devices.reshape(4, 8, mesh.shape["head"]), ("seq_0", "seq_1", "head"))
    in_specs = (
        P(None, SEQ, "head"),
        P(SEQ, "head"),
        P(None, "head", SEQ),
        P(None, "head"),
        P(None, None, "head"),
        P(None, "head", None),
    )
    out_specs = P(SEQ, "head")
    return jax.shard_map(
        shards, mesh=split, in_specs=in_specs, out_specs=out_specs, check_vma=False
    )
```

profile of v0, /device:TPU:1, one launch (start us, length us, event | category | flops | bytes accessed | tf_op | source)
XLA Modules:
  0.0 267.7 jit_solution(604900775022704233)
XLA Ops:
  0.0 1.0 convert_element_type.41
  1.0 0.8 fusion.311
  1.9 1.3 fusion.314
  3.3 0.6 broadcast.596
  3.8 2.5 fusion.310
  7.1 0.5 reduce_window_sum.24
  9.6 0.4 copy-done.11
  11.4 0.6 fusion.312
  13.4 0.4 convolution_bitcast_fusion.11
  14.1 0.7 fusion.313
  14.8 0.4 fusion.87
  15.2 0.9 while.101
  16.2 21.8 %all-gather.4 = f32[8,128,128]{2,1,0:T(8,128)S(1)} all-gather(f32[1,128,128]{2,1,0:T(8,128)S(1)} %get-tuple-element.769), channel_id=6, replica_groups=mesh['seq_0'=4,'seq_1'=8,'head'=16] {'seq_1'}, dimensions={0}, use_global_device_ids=true | all-gather | bytes 589824 | tf_op jit(solution)/shard_map/all_gather | solution.py:26
  37.9 0.7 copy.174
  38.6 19.8 %all-gather.6 = f32[8,128,128]{2,1,0:T(8,128)S(1)} all-gather(f32[1,128,128]{2,1,0:T(8,128)S(1)} %get-tuple-element.776), channel_id=8, replica_groups=mesh['seq_0'=4,'seq_1'=8,'head'=16] {'seq_1'}, dimensions={0}, use_global_device_ids=true | all-gather | bytes 589824 | tf_op jit(solution)/shard_map/all_gather | solution.py:26
  60.3 9.7 %all-gather.7 = f32[512,128]{1,0:T(8,128)S(1)} all-gather(f32[128,128]{1,0:T(8,128)S(1)} %convolution_add_fusion.28), channel_id=9, replica_groups=mesh['seq_0'=4,'seq_1'=8,'head'=16] {'seq_0'}, dimensions={0}, use_global_device_ids=true | all-gather | bytes 327680 | tf_op jit(solution)/shard_map/all_gather | solution.py:26
  71.6 9.4 %all-gather.5 = f32[512,128]{1,0:T(8,128)S(1)} all-gather(f32[128,128]{1,0:T(8,128)S(1)} %fusion.187), channel_id=7, replica_groups=mesh['seq_0'=4,'seq_1'=8,'head'=16] {'seq_0'}, dimensions={0}, use_global_device_ids=true | all-gather | bytes 327680 | tf_op jit(solution)/shard_map/all_gather | solution.py:26
  82.8 0.6 copy-done.13
  83.6 0.6 broadcast.515.clone.2
  84.2 0.6 broadcast.515.clone.3
  84.9 8.6 %while.103 = (s32[]{:T(128)}, f32[1,128,128]{2,1,0:T(8,128)S(1)}, f32[2,128,128]{2,1,0:T(8,128)S(1)}, f32[2,64,128]{2,1,0:T(8,128)}, f32[2,64,128]{2,1,0:T(8,128...) while((s32[]{:T(128)}, f32[1,128,128]{2,1,0:T(8,128)S(1)}, ...), condition=%wide.region_10.11_spmd, body=%wide.region_9.10_spmd.sunk | while | flops 25206784 | bytes 1018065 | solution.py:115
  85.1 0.6 bitcast_dynamic-update-slice_fusion.26
  85.7 1.2 constant_dynamic-slice_fusion.9
  87.0 0.8 fusion.475
  87.8 0.7 dynamic_update_slice.163
  88.5 0.6 bitcast_dynamic-update-slice_fusion.24
  89.4 0.6 bitcast_dynamic-update-slice_fusion.26
  90.0 1.2 constant_dynamic-slice_fusion.9
  91.2 0.8 fusion.475
  92.1 0.7 dynamic_update_slice.163
  92.8 0.6 bitcast_dynamic-update-slice_fusion.24
  93.6 4.0 %while.102 = (s32[]{:T(128)}, f32[2,64,128]{2,1,0:T(8,128)S(1)}, f32[2,64,128]{2,1,0:T(8,128)S(1)}, f32[2,64,64]{2,1,0:T(8,128)S(1)}, f32[2,1,1,1]{0,3,2,1:T(1,1...) while((s32[]{:T(128)}, f32[2,64,128]{2,1,0:T(8,128)S(1)}, ...), condition=%wide.region_6.7_spmd, body=%wide.region_5.6_spmd.sunk | while | flops 2 | bytes 327841 | solution.py:115
  93.6 1.2 constant_dynamic-slice_fusion.8
  94.8 0.7 dynamic_update_slice.156
  95.6 1.2 constant_dynamic-slice_fusion.8
  96.8 0.7 dynamic_update_slice.156
  97.6 4.9 %while.105 = (s32[]{:T(128)}, f32[1,128,128]{2,1,0:T(8,128)S(1)}, f32[2,1,1,1]{0,3,2,1:T(1,128)S(1)}, f32[2,64,128]{2,1,0:T(8,128)S(1)}, f32[2,1,64,128]{3,2,1,0...) while((s32[]{:T(128)}, f32[1,128,128]{2,1,0:T(8,128)S(1)}, ...), condition=%wide.region_8.9_spmd.clone, body=%wide.region_7.8_spmd.clone.sunk | while | flops 44138500 | bytes 690835 | solution.py:115
  98.4 0.7 constant_dynamic-slice_fusion.11
  99.1 1.0 fusion.507
  100.9 0.7 constant_dynamic-slice_fusion.11
  101.6 1.0 fusion.507
  102.5 19.5 %all-gather.2 = f32[8,128,128]{2,1,0:T(8,128)S(1)} all-gather(f32[1,128,128]{2,1,0:T(8,128)S(1)} %get-tuple-element.775), channel_id=4, replica_groups=mesh['seq_0'=4,'seq_1'=8,'head'=16] {'seq_1'}, dimensions={0}, use_global_device_ids=true | all-gather | bytes 589824 | tf_op jit(solution)/shard_map/all_gather | solution.py:26
  122.1 20.4 %all-gather = f32[8,128,128]{2,1,0:T(8,128)S(1)} all-gather(f32[1,128,128]{2,1,0:T(8,128)S(1)} %bitcast.764), channel_id=2, replica_groups=mesh['seq_0'=4,'seq_1'=8,'head'=16] {'seq_1'}, dimensions={0}, use_global_device_ids=true | all-gather | bytes 589824 | tf_op jit(solution)/shard_map/all_gather | solution.py:26
  144.3 9.7 %all-gather.3 = f32[512,128]{1,0:T(8,128)S(1)} all-gather(f32[128,128]{1,0:T(8,128)S(1)} %convolution_add_fusion.41), channel_id=5, replica_groups=mesh['seq_0'=4,'seq_1'=8,'head'=16] {'seq_0'}, dimensions={0}, use_global_device_ids=true | all-gather | bytes 327680 | tf_op jit(solution)/shard_map/all_gather | solution.py:26
  155.5 9.8 %all-gather.1 = f32[512,128]{1,0:T(8,128)S(1)} all-gather(f32[128,128]{1,0:T(8,128)S(1)} %fusion.180), channel_id=3, replica_groups=mesh['seq_0'=4,'seq_1'=8,'head'=16] {'seq_0'}, dimensions={0}, use_global_device_ids=true | all-gather | bytes 327680 | tf_op jit(solution)/shard_map/all_gather | solution.py:26
  166.8 14.5 %while.104 = (s32[]{:T(128)}, f32[1,128,128]{2,1,0:T(8,128)S(1)}, f32[2,1,64,128]{3,2,1,0:T(8,128)S(1)}, f32[2,1,64,128]{3,2,1,0:T(8,128)S(1)}, f32[2,1,64,64]{2...) while((s32[]{:T(128)}, f32[1,128,128]{2,1,0:T(8,128)S(1)}, ...), condition=%wide.region_13.14_spmd, body=%wide.region_11.13_spmd.sunk | while | flops 88186880 | bytes 1351905 | solution.py:115
  167.4 1.0 convolution_bitcast_fusion.20
  168.7 1.5 fusion.496
  170.2 0.7 constant_dynamic-slice_fusion.10
  170.9 1.7 fusion.491
  172.9 0.8 dynamic_update_slice.169
  174.6 1.0 convolution_bitcast_fusion.20
  175.9 1.5 fusion.496
  177.5 0.7 constant_dynamic-slice_fusion.10
  178.1 1.7 fusion.491
  180.1 0.7 dynamic_update_slice.169
  188.1 0.4 convolution_bitcast_fusion.13
  189.8 0.9 reduce_window_sum.26
  190.8 0.6 exponential_multiply_fusion
  191.4 0.4 broadcast_multiply_fusion
  192.5 0.6 convolution_bitcast_fusion.10
  193.2 0.6 fusion.86
  193.9 73.1 %all_to_all.5 = f32[16,128,128]{2,1,0:T(8,128)S(1)} all-to-all(f32[16,128,128]{2,1,0:T(8,128)S(1)} %bitcast.743), channel_id=1, replica_groups=mesh['seq_0'=4,'seq_1'=8,'head'=16] {'head'}, dimensions={0} | all-to-all | bytes 2097152 | tf_op jit(solution)/shard_map/all_to_all | solution.py:44
  267.0 0.7 reduce_sum.199
  (268 shorter events, 29.2 us)
Async XLA Ops:
  0.0 192.5 %copy-start = (bf16[3,2048,128]{2,1,0:T(8,128)(2,1)S(1)}, bf16[3,2048,128]{2,1,0:T(8,128)(2,1)}, u32[]{:S(2)}) copy-start(bf16[3,2048,128]{2,1,0:T(8,128)(2,1)} %param.20) | copy-start | bytes 4718596
  1.8 11.5 %copy-start.1 = (f32[1,128,128]{2,1,0:T(8,128)}, f32[1,128,128]{2,1,0:T(8,128)S(1)}, u32[]{:S(2)}) copy-start(f32[1,128,128]{2,1,0:T(8,128)S(1)} %get-tuple-element.1098) | copy-start | bytes 196612
  1.9 7.2 %copy-start.17 = (pred[64,64]{0,1:T(8,128)(4,1)}, pred[64,64]{0,1:T(8,128)(4,1)S(1)}, u32[]{:S(2)}) copy-start(pred[64,64]{0,1:T(8,128)(4,1)S(1)} %iota_compare_fusion.9) | copy-start | bytes 12292
  1.9 7.2 %copy-start.15 = (f32[64,64]{0,1:T(8,128)}, f32[64,64]{0,1:T(8,128)S(1)}, u32[]{:S(2)}) copy-start(f32[64,64]{0,1:T(8,128)S(1)} %fusion.252) | copy-start | bytes 49156
  7.8 4.4 %copy-start.38 = (f32[2]{0:T(128)}, f32[2]{0:T(128)S(1)}, u32[]{:S(2)}) copy-start(f32[2]{0:T(128)S(1)} %slice_reduce_fusion) | copy-start | bytes 28
  8.0 3.1 %copy-start.35 = (f32[128]{0:T(128)}, f32[128]{0:T(128)S(1)}, u32[]{:S(2)}) copy-start(f32[128]{0:T(128)S(1)} %get-tuple-element.968) | copy-start | bytes 1540
  8.0 4.0 %copy-start.33 = (f32[128]{0:T(128)}, f32[128]{0:T(128)S(1)}, u32[]{:S(2)}) copy-start(f32[128]{0:T(128)S(1)} %get-tuple-element.967) | copy-start | bytes 1540
  8.0 3.1 %copy-start.40 = (f32[128]{0:T(128)}, f32[128]{0:T(128)S(1)}, u32[]{:S(2)}) copy-start(f32[128]{0:T(128)S(1)} %add_rsqrt_fusion.1) | copy-start | bytes 1540
  8.2 5.6 %copy-start.20 = (f32[2,64]{1,0:T(2,128)}, f32[2,64]{1,0:T(2,128)S(1)}, u32[]{:S(2)}) copy-start(f32[2,64]{1,0:T(2,128)S(1)} %div.45) | copy-start | bytes 1540
  9.4 0.6 copy-start.11
  10.4 1.7 copy-start.7
  10.9 1.4 copy-start.9
  11.1 2.7 %copy-start.5 = (f32[2,64,64]{2,1,0:T(8,128)}, f32[2,64,64]{2,1,0:T(8,128)S(1)}, u32[]{:S(2)}) copy-start(f32[2,64,64]{2,1,0:T(8,128)S(1)} %fusion.318) | copy-start | bytes 98308
  11.4 1.6 copy-start.3
  12.0 0.6 copy-start.28
  12.0 2.8 %copy-start.26 = (f32[2,64]{1,0:T(2,128)}, f32[2,64]{1,0:T(2,128)S(1)}, u32[]{:S(2)}) copy-start(f32[2,64]{1,0:T(2,128)S(1)} %get-tuple-element.1105) | copy-start | bytes 1540
  12.1 0.6 copy-start.23
  71.3 11.1 %copy-start.24 = (f32[2,64]{1,0:T(2,128)S(1)}, f32[2,64]{1,0:T(2,128)}, u32[]{:S(2)}) copy-start(f32[2,64]{1,0:T(2,128)} %copy-done.23) | copy-start | bytes 1540
  82.8 0.6 copy-start.13
  93.5 4.1 %copy-start.22 = (bf16[128,128]{1,0:T(8,128)(2,1)S(1)}, bf16[128,128]{1,0:T(8,128)(2,1)}, u32[]{:S(2)}) copy-start(bf16[128,128]{1,0:T(8,128)(2,1)} %param.17) | copy-start | bytes 98308
  97.6 24.5 %copy-start.19 = (f32[1,128,128]{1,2,0:T(8,128)S(1)}, f32[1,128,128]{1,2,0:T(8,128)}, u32[]{:S(2)}) copy-start(f32[1,128,128]{1,2,0:T(8,128)} %copy.174) | copy-start | bytes 196612
  166.8 14.8 %copy-start.27 = (f32[2,64]{1,0:T(2,128)S(1)}, f32[2,64]{1,0:T(2,128)}, u32[]{:S(2)}) copy-start(f32[2,64]{1,0:T(2,128)} %copy-done.26) | copy-start | bytes 1540
  166.8 15.1 %copy-start.2 = (f32[1,128,128]{2,1,0:T(8,128)S(1)}, f32[1,128,128]{2,1,0:T(8,128)}, u32[]{:S(2)}) copy-start(f32[1,128,128]{2,1,0:T(8,128)} %copy-done.1) | copy-start | bytes 196612
  166.8 15.1 %copy-start.21 = (f32[2,64]{1,0:T(2,128)S(1)}, f32[2,64]{1,0:T(2,128)}, u32[]{:S(2)}) copy-start(f32[2,64]{1,0:T(2,128)} %copy-done.20) | copy-start | bytes 1540
  166.8 15.4 %copy-start.6 = (f32[2,64,64]{2,1,0:T(8,128)S(1)}, f32[2,64,64]{2,1,0:T(8,128)}, u32[]{:S(2)}) copy-start(f32[2,64,64]{2,1,0:T(8,128)} %copy-done.5) | copy-start | bytes 98308
  166.8 15.6 %copy-start.4 = (f32[2,64,64]{1,2,0:T(8,128)S(1)}, f32[2,64,64]{1,2,0:T(8,128)}, u32[]{:S(2)}) copy-start(f32[2,64,64]{1,2,0:T(8,128)} %copy-done.3) | copy-start | bytes 98308
  181.3 2.9 %copy-start.10 = (f32[2,64,64]{1,2,0:T(8,128)S(1)}, f32[2,64,64]{1,2,0:T(8,128)}, u32[]{:S(2)}) copy-start(f32[2,64,64]{1,2,0:T(8,128)} %copy-done.9) | copy-start | bytes 98308
  181.3 3.6 %copy-start.8 = (f32[2,64,64]{1,2,0:T(8,128)S(1)}, f32[2,64,64]{1,2,0:T(8,128)}, u32[]{:S(2)}) copy-start(f32[2,64,64]{1,2,0:T(8,128)} %copy-done.7) | copy-start | bytes 98308
  182.2 3.6 %copy-start.12 = (f32[2,64,64]{1,2,0:T(8,128)S(1)}, f32[2,64,64]{1,2,0:T(8,128)}, u32[]{:S(2)}) copy-start(f32[2,64,64]{1,2,0:T(8,128)} %copy-done.11) | copy-start | bytes 98308
  183.0 3.6 %copy-start.16 = (f32[64,64]{0,1:T(8,128)S(1)}, f32[64,64]{0,1:T(8,128)}, u32[]{:S(2)}) copy-start(f32[64,64]{0,1:T(8,128)} %copy-done.15) | copy-start | bytes 49156
  183.0 3.6 %copy-start.18 = (pred[64,64]{0,1:T(8,128)(4,1)S(1)}, pred[64,64]{0,1:T(8,128)(4,1)}, u32[]{:S(2)}) copy-start(pred[64,64]{0,1:T(8,128)(4,1)} %copy-done.17) | copy-start | bytes 12292
  183.9 3.7 %copy-start.14 = (f32[2,64,64]{1,2,0:T(8,128)S(1)}, f32[2,64,64]{1,2,0:T(8,128)}, u32[]{:S(2)}) copy-start(f32[2,64,64]{1,2,0:T(8,128)} %copy-done.13) | copy-start | bytes 98308
  185.2 3.5 %copy-start.25 = (f32[2,64]{1,0:T(2,128)S(1)}, f32[2,64]{1,0:T(2,128)}, u32[]{:S(2)}) copy-start(f32[2,64]{1,0:T(2,128)} %copy-done.23) | copy-start | bytes 1540
  185.5 3.5 %copy-start.29 = (f32[2,64]{1,0:T(2,128)S(1)}, f32[2,64]{1,0:T(2,128)}, u32[]{:S(2)}) copy-start(f32[2,64]{1,0:T(2,128)} %copy-done.28) | copy-start | bytes 1540
  185.5 3.8 %copy-start.37 = (f32[1,1,128]{2,1,0:T(1,128)S(1)}, f32[1,1,128]{2,1,0:T(1,128)}, u32[]{:S(2)}) copy-start(f32[1,1,128]{2,1,0:T(1,128)} %get-tuple-element.1086) | copy-start | bytes 1540
  185.5 3.9 %copy-start.39 = (f32[2]{0:T(128)S(1)}, f32[2]{0:T(128)}, u32[]{:S(2)}) copy-start(f32[2]{0:T(128)} %copy-done.38) | copy-start | bytes 28
  185.5 5.2 %copy-start.32 = (f32[2,1,128]{2,1,0:T(1,128)S(1)}, f32[2,1,128]{2,1,0:T(1,128)}, u32[]{:S(2)}) copy-start(f32[2,1,128]{2,1,0:T(1,128)} %param.18) | copy-start | bytes 3076
  185.6 5.9 %copy-start.31 = (f32[2,64]{1,0:T(2,128)S(1)}, f32[2,64]{1,0:T(2,128)}, u32[]{:S(2)}) copy-start(f32[2,64]{1,0:T(2,128)} %get-tuple-element.1104) | copy-start | bytes 1540
  186.6 5.6 %copy-start.34 = (f32[128]{0:T(128)S(1)}, f32[128]{0:T(128)}, u32[]{:S(2)}) copy-start(f32[128]{0:T(128)} %copy-done.33) | copy-start | bytes 1540
  186.6 5.6 %copy-start.36 = (f32[128]{0:T(128)S(1)}, f32[128]{0:T(128)}, u32[]{:S(2)}) copy-start(f32[128]{0:T(128)} %copy-done.35) | copy-start | bytes 1540
  186.6 5.6 %copy-start.41 = (f32[128]{0:T(128)S(1)}, f32[128]{0:T(128)}, u32[]{:S(2)}) copy-start(f32[128]{0:T(128)} %copy-done.40) | copy-start | bytes 1540
  192.2 0.9 copy-start.30
where the time goes:
time: 269 us; the launch traced here: 268 us
  blocking collectives  193 us (72%)
  matrix products  37.6 us (14%)
  local copies, waits for them, and re-layouts  23.1 us (9%)
  other arithmetic  11.1 us (4%)
    all_gather x8, blocking collectives, carried_in(): pieces = jax.tree.map(lambda part: lax.all_gather(part, axis), running)  120 us
    all_to_all x1, blocking collectives, summed_on_arrival(): lax.all_to_all(pieces, axis, split_axis=0, concat_axis=0, tiled=True)  73.1 us
    dot_general x122, matrix products, matmul(): return jnp.matmul(left, right, precision=exact_precision)  36.3 us
    dynamic_slice x8, local copies, waits for them, and re-layouts, block_run(): final_state, out_rows = lax.scan(block_step, start_state, pieces)  7.53 us
    dynamic_update_slice x22, local copies, waits for them, and re-layouts, block_run(): final_state, out_rows = lax.scan(block_step, start_state, pieces)  6.96 us

commit v1 on v0

v1 whole, which is shorter than its diff:
```python
import functools

import jax
import jax.numpy as jnp
from jax import lax
from jax.experimental import pallas as pl
from jax.experimental.pallas import tpu as pltpu
from jax.sharding import PartitionSpec as P

DK = 128
ROW = 8
f32, bf16 = jnp.float32, jnp.bfloat16
MESH = pl.DeviceIdType.MESH


def split(a):
    high = a.astype(bf16)
    return high, (a - high.astype(f32)).astype(bf16)


def dot(a, b, contract_b):
    return lax.dot_general(
        a, b, (((1,), (contract_b,)), ((), ())), preferred_element_type=f32
    )


def folded(out):
    half = out.shape[1] // 2
    return out[:, :half] + out[:, half:]


def mm(a, b):
    ah, al = split(a)
    bh, bl = split(b)
    right = jnp.concatenate([bh, bl], 1)
    return folded(dot(jnp.concatenate([ah, al], 1), jnp.concatenate([right, right], 0), 0))


def mm_nt(a, b):
    ah, al = split(a)
    bh, bl = split(b)
    right = jnp.concatenate(
        [jnp.concatenate([bh, bh], 1), jnp.concatenate([bl, bl], 1)], 0
    )
    return folded(dot(jnp.concatenate([ah, al], 1), right, 1))


def row_sum(a):
    return jnp.sum(a, axis=1, keepdims=True)


def col_sum(a):
    return jnp.sum(a, axis=0, keepdims=True)


def sigmoid(a):
    return 1.0 / (1.0 + jnp.exp(-a))


def softplus(a):
    return jnp.maximum(a, 0.0) + jnp.log1p(jnp.exp(-jnp.abs(a)))


def indices(n=DK):
    return (
        lax.broadcasted_iota(jnp.int32, (n, n), 0),
        lax.broadcasted_iota(jnp.int32, (n, n), 1),
    )


def inverse_of(lower, row, col):
    eye = jnp.where(row == col, 1.0, 0.0)
    inner = jnp.where((row // 16) == (col // 16), lower, 0.0)
    total = eye - inner
    power = mm(inner, inner)
    total = total + mm(total, power)
    power = mm(power, power)
    total = total + mm(total, power)
    power = mm(power, power)
    total = total + mm(total, power)
    for size in (16, 32):
        cross = jnp.where(
            ((row // (2 * size)) == (col // (2 * size))) & ((row // size) != (col // size)),
            lower,
            0.0,
        )
        total = total - mm(total, mm(cross, total))
    cross = jnp.where((row // 64) != (col // 64), lower, 0.0)
    return total, mm(total, cross)


def kernel(
    nx,
    nz,
    proj_ref,
    do_ref,
    logit_ref,
    hp_ref,
    w_hbm,
    gate_ref,
    out_ref,
    sv,
    cols,
    m_all,
    bf_own,
    bf_all,
    pre,
    suf,
    xf_send,
    xf_recv,
    xb_send,
    xb_recv,
    sg_send,
    sg_all,
    wv,
    own,
    pair_send,
    pair_recv,
    zp_send,
    zp_recv,
    zm_send,
    zm_recv,
    w_sem,
    ag_ss,
    ag_rs,
    a1_ss,
    a1_rs,
    x_ss,
    x_rs,
    a2_ss,
    a2_rs,
    p_ss,
    p_rs,
    zp_ss,
    zp_rs,
    zm_ss,
    zm_rs,
):
    ny, sl = ROW, DK // ROW
    s, h = lax.axis_index("seq"), lax.axis_index("head")
    x, y = s // ny, lax.rem(s, ny)
    z, c = h // 2, lax.rem(h, 2)

    def in_row(d):
        return lax.rem(y + d, ny)

    def row_peer(d):
        return (x * ny + in_row(d), h)

    def x_peer(d):
        return (lax.rem(x + d + nx, nx) * ny + y, h)

    def z_peer(d):
        return (s, lax.rem(z + d + nz, nz) * 2 + c)

    partner = (s, z * 2 + 1 - c)

    def send(src, dst, ss, rs, dev):
        copy = pltpu.make_async_remote_copy(
            src_ref=src, dst_ref=dst, send_sem=ss, recv_sem=rs, device_id=dev, device_id_type=MESH
        )
        copy.start()
        return copy

    w_copy = pltpu.make_async_copy(w_hbm, wv, w_sem)
    w_copy.start()
    barrier = pltpu.get_barrier_semaphore()
    greeted = [row_peer(d) for d in range(1, ny)] + [x_peer(1), x_peer(-1), partner]
    greeted += [z_peer(1), z_peer(-1)]
    for dev in greeted:
        pl.semaphore_signal(barrier, inc=1, device_id=dev, device_id_type=MESH)

    row, col = indices()
    eye = row == col

    def to_col(r):
        return row_sum(jnp.where(eye, r, 0.0))

    def to_row(v):
        return col_sum(jnp.where(eye, v, 0.0))

    hp = hp_ref[...]
    rate = jnp.exp(hp[0:1, 0:1])
    arg = logit_ref[0] + hp[1:2, 0:1]
    decay_row = -rate * softplus(arg)
    beta_row = sigmoid(logit_ref[1])
    beta = to_col(beta_row)
    g = row_sum(jnp.where(col <= row, decay_row, 0.0))
    g_row = to_row(g)
    g_last = g_row[:, DK - 1 : DK]
    lower, upper = row >= col, row <= col
    ratio = jnp.where(lower, jnp.exp(jnp.where(lower, g - g_row, 0.0)), 0.0)
    ratio_t = jnp.where(upper, jnp.exp(jnp.where(upper, g_row - g, 0.0)), 0.0)
    grown = jnp.exp(g)
    rest = jnp.exp(g_last - g)
    last = jnp.exp(g_last)
    k_raw = proj_ref[1].astype(f32)
    k_scale = lax.rsqrt(row_sum(k_raw * k_raw) + 1.0)
    k = k_raw * k_scale
    inner = mm_nt(k, k)
    bare = jnp.where(row > col, ratio * inner, 0.0)
    lo = bare * beta
    half, crossed = inverse_of(lo, row, col)
    y_in = (beta * grown) * k
    half_y = mm(half, y_in)
    w = half_y - mm(crossed, half_y)
    k_end = rest * k
    k_end_t = k_end.T
    m_own = jnp.where(eye, last, 0.0) - mm(k_end_t, w)
    m_all[y] = m_own

    pl.semaphore_wait(barrier, len(greeted))
    ag = [
        send(m_all.at[y], m_all.at[y], ag_ss.at[d], ag_rs.at[d], row_peer(d))
        for d in (4, 3, 5, 2, 6, 1, 7)
    ]

    q_raw = proj_ref[0].astype(f32)
    q_scale = lax.rsqrt(row_sum(q_raw * q_raw) + 1.0)
    qn = q_raw * q_scale
    q = qn * (DK ** (-0.5))
    v = proj_ref[2].astype(f32)
    do = do_ref[...].astype(f32)
    inv = half - mm(crossed, half)
    att = ratio * mm_nt(q, k)
    q_grown = grown * q
    f_off = mm(do.T, q_grown - mm(att, w))
    u = mm(inv, beta * v)
    b_off = mm(u.T, k_end)
    bf_own[:, 0] = b_off.reshape(ny, sl, DK)
    bf_own[:, 1] = f_off.reshape(ny, sl, DK)
    a1 = [
        send(bf_own.at[in_row(d)], bf_all.at[y], a1_ss.at[d], a1_rs.at[d], row_peer(d))
        for d in range(1, ny)
    ]
    bf_all[y] = bf_own[y]
    att_t = ratio_t * mm_nt(k, q)
    saved = (u, w, mm(att_t, do), k_end, inv.T, ratio, ratio_t, bare, lo, att, att_t, k, qn, y_in)
    for n, value in enumerate(saved):
        sv[n] = value
    sv[len(saved)] = jnp.where(row < col, ratio_t * inner * beta_row, 0.0)
    sig = to_col(sigmoid(arg))
    for n, value in enumerate((beta, grown, rest, k_scale, q_scale, sig)):
        cols[n] = jnp.broadcast_to(value, (DK, DK))

    for copy in ag:
        copy.wait_recv()
    for copy in a1:
        copy.wait_recv()

    zeros = jnp.zeros((sl, DK), f32)
    pad = jnp.zeros((DK, DK), f32)
    start = jnp.concatenate([zeros, jnp.where(eye, 1.0, 0.0)], 0)
    fwd = bwd = start
    for n in range(ny):
        j, i = n, ny - 1 - n
        pre[j] = fwd
        suf[i] = bwd
        fwd = mm_nt(fwd, m_all[j]) + jnp.concatenate([bf_all[j, 0], pad], 0)
        bwd = mm(bwd, m_all[i]) + jnp.concatenate([bf_all[i, 1], pad], 0)

    s_row = g_row_in = zeros
    xs = []
    for n in range(nx - 1):
        if n == 0:
            s_out, g_out = fwd[:sl], bwd[:sl]
        else:
            s_out = mm(s_row, fwd[sl:]) + fwd[:sl]
            g_out = mm(g_row_in, bwd[sl:]) + bwd[:sl]
        xf_send[n] = s_out
        xb_send[n] = g_out
        cf = send(xf_send.at[n], xf_recv.at[n], x_ss.at[0, n], x_rs.at[0, n], x_peer(1))
        cb = send(xb_send.at[n], xb_recv.at[n], x_ss.at[1, n], x_rs.at[1, n], x_peer(-1))
        xs += [cf, cb]
        cf.wait_recv()
        cb.wait_recv()
        s_row = jnp.where(x > 0, xf_recv[n], 0.0)
        g_row_in = jnp.where(x < nx - 1, xb_recv[n], 0.0)

    for j in range(ny):
        sg_send[j, 0] = mm(s_row, pre[j, sl:]) + pre[j, :sl]
        sg_send[j, 1] = mm(g_row_in, suf[j, sl:]) + suf[j, :sl]
    a2 = [
        send(sg_send.at[in_row(d)], sg_all.at[y], a2_ss.at[d], a2_rs.at[d], row_peer(d))
        for d in (4, 3, 5, 2, 6, 1, 7)
    ]
    sg_all[y] = sg_send[y]
    for copy in a2:
        copy.wait_recv()
    st = sg_all[:, 0].reshape(DK, DK)
    gt = sg_all[:, 1].reshape(DK, DK)

    u, w, att_do, k_end, inv_t, ratio, ratio_t = (sv[n] for n in range(7))
    fresh = u - mm_nt(w, st)
    d_fresh = att_do + mm_nt(k_end, gt)
    do = do_ref[...].astype(f32)
    d_qg = mm(do, st)
    dx = mm(inv_t, d_fresh)
    d_ke = mm(fresh, gt)
    d_att = jnp.where(lower, mm_nt(do, fresh), 0.0)
    d_att_t = jnp.where(upper, mm_nt(fresh, do), 0.0)
    dy = -mm(dx, st)
    d_lo = jnp.where(row > col, -mm_nt(dx, fresh), 0.0)
    d_lo_t = jnp.where(row < col, -mm_nt(fresh, dx), 0.0)
    bare, lo, att, att_t, k, qn, y_in, lo_t = (sv[n] for n in range(7, 15))
    beta, grown, rest, k_scale, q_scale, sig = (cols[n] for n in range(6))
    q = qn * (DK ** (-0.5))
    v = proj_ref[2].astype(f32)
    sym = d_lo * ratio * beta + d_lo_t * ratio_t * beta_row
    dq = mm(d_att * ratio, k) + grown * d_qg
    dk = mm(d_att_t * ratio_t, q) + mm(sym, k) + (beta * grown) * dy + rest * d_ke
    ke_part = d_ke * k_end
    d_beta = row_sum(d_lo * bare + dx * v + grown * dy * k)
    mixed = d_lo * lo - d_lo_t * lo_t + d_att * att - d_att_t * att_t
    mixed = mixed + dy * y_in + d_qg * (grown * q) - ke_part
    dg_row = to_row(row_sum(mixed))
    tail = col_sum(row_sum(ke_part + last * (st * gt)))
    d_decay = row_sum(jnp.where(col >= row, dg_row, 0.0)) + tail
    d_l0 = -rate * sig * d_decay
    d_l1 = d_beta * beta * (1.0 - beta)
    dq = (q_scale * (DK ** (-0.5))) * (dq - qn * row_sum(dq * qn))
    dk = k_scale * (dk - k * row_sum(dk * k))
    dqk = jnp.concatenate([dq.astype(bf16), dk.astype(bf16)], 1)
    dv = (beta * dx).astype(bf16)

    w_copy.wait()

    def term(target, core):
        at = pl.multiple_of(target * (2 * DK) + core * DK, DK)
        here = pl.ds(at, DK)
        both = jnp.concatenate([wv[0, here, :], wv[1, here, :]], 1)
        out = dot(dqk, both, 1) + dot(dv, wv[2, here, :], 1)
        out = out + d_l0 * gate_ref[0, :, here].astype(f32)
        return out + d_l1 * gate_ref[1, :, here].astype(f32)

    plus, minus = nz // 2, (nz - 1) // 2
    order = []
    for n in range(plus):
        order.append(plus - n)
        if n < minus:
            order.append(nz - minus + n)
    order.append(0)
    pairs = {}
    for d in order:
        target = lax.rem(z + d, nz)
        pair_send[d] = term(target, 1 - c)
        pairs[d] = send(pair_send.at[d], pair_recv.at[d], p_ss.at[d], p_rs.at[d], partner)
        own[d] = term(target, c)
    zs = []
    last_p = last_m = None
    for n in range(plus):
        d = plus - n
        pairs[d].wait_recv()
        value = own[d] + pair_recv[d]
        if last_p is not None:
            last_p.wait_recv()
            value = value + zp_recv[n - 1]
        zp_send[n] = value
        last_p = send(zp_send.at[n], zp_recv.at[n], zp_ss.at[n], zp_rs.at[n], z_peer(1))
        zs.append(last_p)
        if n < minus:
            d = nz - minus + n
            pairs[d].wait_recv()
            value = own[d] + pair_recv[d]
            if last_m is not None:
                last_m.wait_recv()
                value = value + zm_recv[n - 1]
            zm_send[n] = value
            last_m = send(zm_send.at[n], zm_recv.at[n], zm_ss.at[n], zm_rs.at[n], z_peer(-1))
            zs.append(last_m)
    pairs[0].wait_recv()
    total = own[0] + pair_recv[0]
    if last_m is not None:
        last_m.wait_recv()
        total = total + zm_recv[minus - 1]
    last_p.wait_recv()
    out_ref[...] = (total + zp_recv[plus - 1]).astype(bf16)
    for copy in ag + a1 + xs + a2 + list(pairs.values()) + zs:
        copy.wait_send()


def shards(nx, nz, projected, out_grad, logits, head_params, qkv_weight, gate_weight):
    vm = pl.BlockSpec(memory_space=pltpu.VMEM)
    sl, ny = DK // ROW, ROW
    plus, minus = nz // 2, max((nz - 1) // 2, 1)
    dma = pltpu.SemaphoreType.DMA
    scratch = [
        pltpu.VMEM((15, DK, DK), f32),
        pltpu.VMEM((6, DK, DK), f32),
        pltpu.VMEM((ny, DK, DK), f32),
        pltpu.VMEM((ny, 2, sl, DK), f32),
        pltpu.VMEM((ny, 2, sl, DK), f32),
        pltpu.VMEM((ny, sl + DK, DK), f32),
        pltpu.VMEM((ny, sl + DK, DK), f32),
        pltpu.VMEM((nx - 1, sl, DK), f32),
        pltpu.VMEM((nx - 1, sl, DK), f32),
        pltpu.VMEM((nx - 1, sl, DK), f32),
        pltpu.VMEM((nx - 1, sl, DK), f32),
        pltpu.VMEM((ny, 2, sl, DK), f32),
        pltpu.VMEM((ny, 2, sl, DK), f32),
        pltpu.VMEM(qkv_weight.shape, bf16),
        pltpu.VMEM((nz, DK, DK), f32),
        pltpu.VMEM((nz, DK, DK), f32),
        pltpu.VMEM((nz, DK, DK), f32),
        pltpu.VMEM((plus, DK, DK), f32),
        pltpu.VMEM((plus, DK, DK), f32),
        pltpu.VMEM((minus, DK, DK), f32),
        pltpu.VMEM((minus, DK, DK), f32),
        dma(()),
        dma((ny,)),
        dma((ny,)),
        dma((ny,)),
        dma((ny,)),
        dma((2, nx - 1)),
        dma((2, nx - 1)),
        dma((ny,)),
        dma((ny,)),
        dma((nz,)),
        dma((nz,)),
        dma((plus,)),
        dma((plus,)),
        dma((minus,)),
        dma((minus,)),
    ]
    return pl.pallas_call(
        functools.partial(kernel, nx, nz),
        out_shape=jax.ShapeDtypeStruct((DK, DK), bf16),
        in_specs=[vm, vm, vm, vm, pl.BlockSpec(memory_space=pl.ANY), vm],
        out_specs=vm,
        scratch_shapes=scratch,
        compiler_params=pltpu.CompilerParams(
            collective_id=0, has_side_effects=True, vmem_limit_bytes=48 * 1024 * 1024
        ),
        name="delta_backward",
    )(projected, out_grad, logits, head_params, qkv_weight, gate_weight)


def solution(mesh):
    nx, nz = mesh.shape["seq"] // ROW, mesh.shape["head"] // 2
    in_specs = (
        P(None, "seq", "head"),
        P("seq", "head"),
        P(None, "head", "seq"),
        P(None, "head"),
        P(None, None, "head"),
        P(None, "head", None),
    )
    return jax.shard_map(
        functools.partial(shards, nx, nz),
        mesh=mesh,
        in_specs=in_specs,
        out_specs=P("seq", "head"),
        check_vma=False,
    )
```

time: 269 us -> 71 us (0.26)
  the two profiles are of different devices: /device:TPU:1 before, /device:TPU:64 now
where the time goes in v1:
time: 71 us; the launch traced here: 70.7 us
  Pallas kernels  64.9 us (91%)
  local copies, waits for them, and re-layouts  5.8 us (8%)
    pallas_call x1, Pallas kernels, shards(): pl.pallas_call(functools.partial(kernel, nx, nz), out_shape=jax.ShapeDtyp...  64.9 us
    unnamed x11, local copies, waits for them, and re-layouts  5.8 us

profile of v1, /device:TPU:64, one launch (start us, length us, event | category | flops | bytes accessed | tf_op | source)
XLA Modules:
  0.0 70.7 jit_solution(5405297715129973494)
XLA Ops:
  0.0 0.7 %copy.7.hp_ref = f32[2,1]{1,0:T(2,128)S(1)} copy(f32[2,1]{0,1:T(1,128)} %param.9) | data formatting | bytes 16 | tf_op args[3]
  0.7 0.7 %copy.8.gate_ref = bf16[2,1,2048]{2,1,0:T(2,128)(2,1)S(1)} copy(bf16[2,1,2048]{2,0,1:T(2,128)(2,1)} %param.11) | data formatting | bytes 16384 | tf_op args[5]
  1.5 0.0 copy-start
  1.5 1.4 %copy-done = bf16[3,2048,128]{2,1,0:T(8,128)(2,1)S(1)} copy-done((bf16[3,2048,128]{2,1,0:T(8,128)(2,1)S(1)}, bf16[3,2048,128]{2,1,0:T(8,128)(2,1)}, u32[]{:S(2)}) %copy-start) | copy-done | bytes 1572888
  2.9 0.0 copy-start.1
  2.9 0.9 %copy-done.1 = bf16[3,128,128]{2,1,0:T(8,128)(2,1)S(1)} copy-done((bf16[3,128,128]{2,1,0:T(8,128)(2,1)S(1)}, bf16[3,128,128]{2,1,0:T(8,128)(2,1)}, u32[]{:S(2)}) %copy-start.1) | copy-done | bytes 98328
  3.8 0.0 copy-start.2
  3.8 0.8 %copy-done.2 = bf16[128,128]{1,0:T(8,128)(2,1)S(1)} copy-done((bf16[128,128]{1,0:T(8,128)(2,1)S(1)}, bf16[128,128]{1,0:T(8,128)(2,1)}, u32[]{:S(2)}) %copy-start.2) | copy-done | bytes 32792
  4.5 0.0 copy-start.3
  4.5 0.7 copy-done.3
  5.2 64.9 %delta_backward.1 = bf16[128,128]{1,0:T(8,128)(2,1)S(1)} custom-call(bf16[3,128,128]{2,1,0:T(8,128)(2,1)S(1)} %copy-done.1, bf16[128,128]{1,0:T(8,128)(2,1)S(1)} %copy-done.2, f32[2,1,128]{2,1,0:T(1,128)S(1)} %copy-done.3, f32[2,1]{1,0:T(2,128)S(1)} %copy.7.hp_ref, bf16[3,2048,128]{2,1,0:T(8,128)(2,1)S(1)} %copy-done, bf16[2,1,2048]{2,1,0:T(2,128)(2,1)S(1)} %copy.8.gate_ref), custom_call_target="tpu_custom_call" | custom-call | tf_op jit(solution)/shard_map/delta_backward/pallas_call | solution.py:425
  70.1 0.6 copy.10
Async XLA Ops:
  1.5 1.4 %copy-start = (bf16[3,2048,128]{2,1,0:T(8,128)(2,1)S(1)}, bf16[3,2048,128]{2,1,0:T(8,128)(2,1)}, u32[]{:S(2)}) copy-start(bf16[3,2048,128]{2,1,0:T(8,128)(2,1)} %w_hbm.1) | copy-start | bytes 4718596
  2.9 0.9 %copy-start.1 = (bf16[3,128,128]{2,1,0:T(8,128)(2,1)S(1)}, bf16[3,128,128]{2,1,0:T(8,128)(2,1)}, u32[]{:S(2)}) copy-start(bf16[3,128,128]{2,1,0:T(8,128)(2,1)} %proj_ref.1) | copy-start | bytes 294916
  3.8 0.8 %copy-start.2 = (bf16[128,128]{1,0:T(8,128)(2,1)S(1)}, bf16[128,128]{1,0:T(8,128)(2,1)}, u32[]{:S(2)}) copy-start(bf16[128,128]{1,0:T(8,128)(2,1)} %do_ref.1) | copy-start | bytes 98308
  4.5 0.7 copy-start.3

commit v2 on v1

v2 whole, which is shorter than its diff:
```python
import functools

import jax
import jax.numpy as jnp
from jax import lax
from jax.experimental import pallas as pl
from jax.experimental.pallas import tpu as pltpu
from jax.sharding import PartitionSpec as P

DK = 128
ROW = 8
HOLD = 4
f32, bf16 = jnp.float32, jnp.bfloat16
MESH = pl.DeviceIdType.MESH


def split(a):
    high = a.astype(bf16)
    return high, (a - high.astype(f32)).astype(bf16)


def dot(a, b, contract_b):
    return lax.dot_general(
        a, b, (((1,), (contract_b,)), ((), ())), preferred_element_type=f32
    )


def folded(out):
    half = out.shape[1] // 2
    return out[:, :half] + out[:, half:]


def mm(a, b):
    ah, al = split(a)
    bh, bl = split(b)
    right = jnp.concatenate([bh, bl], 1)
    return folded(dot(jnp.concatenate([ah, al], 1), jnp.concatenate([right, right], 0), 0))


def mm_nt(a, b):
    ah, al = split(a)
    bh, bl = split(b)
    right = jnp.concatenate(
        [jnp.concatenate([bh, bh], 1), jnp.concatenate([bl, bl], 1)], 0
    )
    return folded(dot(jnp.concatenate([ah, al], 1), right, 1))


def row_sum(a):
    return jnp.sum(a, axis=1, keepdims=True)


def col_sum(a):
    return jnp.sum(a, axis=0, keepdims=True)


def sigmoid(a):
    return 1.0 / (1.0 + jnp.exp(-a))


def softplus(a):
    return jnp.maximum(a, 0.0) + jnp.log1p(jnp.exp(-jnp.abs(a)))


def indices(n=DK):
    return (
        lax.broadcasted_iota(jnp.int32, (n, n), 0),
        lax.broadcasted_iota(jnp.int32, (n, n), 1),
    )


def inverse_of(lower, row, col):
    eye = jnp.where(row == col, 1.0, 0.0)
    inner = jnp.where((row // 16) == (col // 16), lower, 0.0)
    total = eye - inner
    power = mm(inner, inner)
    total = total + mm(total, power)
    power = mm(power, power)
    total = total + mm(total, power)
    power = mm(power, power)
    total = total + mm(total, power)
    for size in (16, 32):
        cross = jnp.where(
            ((row // (2 * size)) == (col // (2 * size))) & ((row // size) != (col // size)),
            lower,
            0.0,
        )
        total = total - mm(total, mm(cross, total))
    cross = jnp.where((row // 64) != (col // 64), lower, 0.0)
    return total, mm(total, cross)


def kernel(
    nx,
    nz,
    proj_hbm,
    do_hbm,
    logit_hbm,
    hp_hbm,
    w_hbm,
    gate_hbm,
    out_ref,
    proj_ref,
    do_ref,
    logit_ref,
    hp_ref,
    gate_ref,
    wv,
    sv,
    cols,
    m_all,
    bf_own,
    bf_all,
    pre,
    suf,
    xm_all,
    xb_own,
    xb_all,
    sg_send,
    sg_all,
    term,
    pair_recv,
    z_send,
    z_recv,
    in_sem,
    ag_ss,
    ag_rs,
    a1_ss,
    a1_rs,
    xm_ss,
    xm_rs,
    xb_ss,
    xb_rs,
    a2_ss,
    a2_rs,
    p_ss,
    p_rs,
    z_ss,
    z_rs,
):
    ny, sl, step = ROW, DK // HOLD, ROW // HOLD
    s, h = lax.axis_index("seq"), lax.axis_index("head")
    x, y = s // ny, lax.rem(s, ny)
    z, c = h // 2, lax.rem(h, 2)
    base = c * (step // 2)
    off = lax.rem(y - base + ny, step)
    holds = off == 0
    slot = lax.rem(y - base + ny, ny) // step

    def row_peer(d):
        return (x * ny + lax.rem(y + d + ny, ny), h)

    def x_peer(d):
        return (lax.rem(x + d, nx) * ny + y, h)

    def z_peer(d):
        return (s, lax.rem(z + d + nz, nz) * 2 + c)

    partner = (s, z * 2 + 1 - c)

    def remote(src, dst, ss, rs, dev):
        return pltpu.make_async_remote_copy(
            src_ref=src, dst_ref=dst, send_sem=ss, recv_sem=rs, device_id=dev, device_id_type=MESH
        )

    barrier = pltpu.get_barrier_semaphore()
    greeted = [row_peer(d) for d in range(1, ny)] + [x_peer(d) for d in range(1, nx)]
    greeted += [partner] + [z_peer(d) for d in (1, -1, 2, -2)]
    for dev in greeted:
        pl.semaphore_signal(barrier, inc=1, device_id=dev, device_id_type=MESH)
    loads = (
        (logit_hbm, logit_ref),
        (hp_hbm, hp_ref),
        (proj_hbm, proj_ref),
        (do_hbm, do_ref),
        (gate_hbm, gate_ref),
        (w_hbm, wv),
    )
    loads = [pltpu.make_async_copy(a, b, in_sem.at[n]) for n, (a, b) in enumerate(loads)]
    for copy in loads:
        copy.start()

    row, col = indices()
    eye = row == col

    def to_col(r):
        return row_sum(jnp.where(eye, r, 0.0))

    def to_row(v):
        return col_sum(jnp.where(eye, v, 0.0))

    loads[0].wait()
    loads[1].wait()
    hp = hp_ref[...]
    rate = jnp.exp(hp[:, 0:1])
    arg = logit_ref[0] + hp[:, 1:2]
    decay_row = -rate * softplus(arg)
    beta_row = sigmoid(logit_ref[1])
    beta = to_col(beta_row)
    g = row_sum(jnp.where(col <= row, decay_row, 0.0))
    g_row = to_row(g)
    g_last = g_row[:, DK - 1 : DK]
    lower, upper = row >= col, row <= col
    ratio = jnp.where(lower, jnp.exp(jnp.where(lower, g - g_row, 0.0)), 0.0)
    ratio_t = jnp.where(upper, jnp.exp(jnp.where(upper, g_row - g, 0.0)), 0.0)
    grown = jnp.exp(g)
    rest = jnp.exp(g_last - g)
    last = jnp.exp(g_last)
    loads[2].wait()
    k_raw = proj_ref[1].astype(f32)
    k_scale = lax.rsqrt(row_sum(k_raw * k_raw) + 1.0)
    k = k_raw * k_scale
    inner = mm_nt(k, k)
    bare = jnp.where(row > col, ratio * inner, 0.0)
    lo = bare * beta
    half, crossed = inverse_of(lo, row, col)
    y_in = (beta * grown) * k
    half_y = mm(half, y_in)
    w = half_y - mm(crossed, half_y)
    k_end = rest * k
    k_end_t = k_end.T
    m_all[y] = jnp.where(eye, last, 0.0) - mm(k_end_t, w)

    pl.semaphore_wait(barrier, len(greeted))
    order = [(HOLD // 2 + n) % HOLD for n in range(HOLD)]

    def to_holders(do):
        for n in order:
            dev = row_peer(step * n - off)
            if n == 0:
                pl.when(jnp.logical_not(holds))(functools.partial(do, n, dev))
            else:
                do(n, dev)

    def from_row(ref, ss, rs):
        for j in range(ny):

            @pl.when(y != j)
            def _():
                remote(ref.at[j], ref.at[j], ss.at[0], rs.at[j], partner).wait_recv()

    def m_copy(n, dev):
        return remote(m_all.at[y], m_all.at[y], ag_ss.at[n], ag_rs.at[y], dev)

    def bf_copy(n, dev):
        to = lax.rem(slot_of(n), HOLD)
        return remote(bf_own.at[to], bf_all.at[y], a1_ss.at[n], a1_rs.at[y], dev)

    def slot_of(n):
        return lax.rem(y + step * n - off - base + ny, ny) // step

    to_holders(lambda n, dev: m_copy(n, dev).start())
    q_raw = proj_ref[0].astype(f32)
    q_scale = lax.rsqrt(row_sum(q_raw * q_raw) + 1.0)
    qn = q_raw * q_scale
    q = qn * (DK ** (-0.5))
    v = proj_ref[2].astype(f32)
    loads[3].wait()
    do = do_ref[...].astype(f32)
    inv = half - mm(crossed, half)
    att = ratio * mm_nt(q, k)
    q_grown = grown * q
    f_off = mm(do.T, q_grown - mm(att, w))
    u = mm(inv, beta * v)
    b_off = mm(u.T, k_end)
    bf_own[:, 0] = b_off.reshape(HOLD, sl, DK)
    bf_own[:, 1] = f_off.reshape(HOLD, sl, DK)
    to_holders(lambda n, dev: bf_copy(n, dev).start())
    bf_all[y] = bf_own[slot]
    att_t = ratio_t * mm_nt(k, q)
    saved = (u, w, mm(att_t, do), k_end, inv.T, ratio, ratio_t, bare, lo, att, att_t, k, qn, y_in)
    for n, value in enumerate(saved):
        sv[n] = value
    sv[len(saved)] = jnp.where(row < col, ratio_t * inner * beta_row, 0.0)
    sig = to_col(sigmoid(arg))
    for n, value in enumerate((beta, grown, rest, k_scale, q_scale, sig)):
        cols[n] = jnp.broadcast_to(value, (DK, DK))
    middle = range(1, nx - 1)

    def xm_copy(d):
        return remote(xm_all.at[x], xm_all.at[x], xm_ss.at[d - 1], xm_rs.at[x], x_peer(d))

    def xb_copy(d):
        at = (x + d) // nx
        return remote(xb_own.at[at], xb_all.at[x], xb_ss.at[d - 1], xb_rs.at[x], x_peer(d))

    in_middle = jnp.logical_and(x > 0, x < nx - 1)
    back = (4, 3, 5, 2, 6, 1, 7) if ny == 8 else tuple(range(1, ny))

    def sg_copy(d):
        to = lax.rem(y + d, ny)
        return remote(sg_send.at[to], sg_all.at[slot], a2_ss.at[d], a2_rs.at[slot], row_peer(d))

    @pl.when(holds)
    def _():
        from_row(m_all, ag_ss, ag_rs)
        from_row(bf_all, a1_ss, a1_rs)
        zeros = jnp.zeros((sl, DK), f32)
        pad = jnp.zeros((DK, DK), f32)
        fwd = bwd = jnp.concatenate([zeros, jnp.where(eye, 1.0, 0.0)], 0)
        for n in range(ny):
            j, i = n, ny - 1 - n
            pre[j] = fwd
            suf[i] = bwd
            fwd = mm_nt(fwd, m_all[j]) + jnp.concatenate([bf_all[j, 0], pad], 0)
            bwd = mm(bwd, m_all[i]) + jnp.concatenate([bf_all[i, 1], pad], 0)
        xm_all[x] = bwd[sl:]
        xb_own[0] = fwd[:sl]
        xb_own[1] = bwd[:sl]
        for d in (2, 1, 3) if nx == 4 else range(1, nx):
            xb_copy(d).start()

        @pl.when(in_middle)
        def _():
            for d in (2, 1, 3) if nx == 4 else range(1, nx):
                xm_copy(d).start()

        xb_all[x] = zeros
        for n in range(nx):

            @pl.when(x != n)
            def _():
                if n in middle:
                    remote(xm_all.at[n], xm_all.at[n], xm_ss.at[0], xm_rs.at[n], partner).wait_recv()
                remote(xb_all.at[n], xb_all.at[n], xb_ss.at[0], xb_rs.at[n], partner).wait_recv()

        s_row = jnp.where(x > 0, xb_all[0], 0.0)
        g_in = jnp.where(x < nx - 1, xb_all[nx - 1], 0.0)
        for n in middle:
            i = nx - 1 - n
            s_row = jnp.where(x > n, mm_nt(s_row, xm_all[n]) + xb_all[n], s_row)
            g_in = jnp.where(x < i, mm(g_in, xm_all[i]) + xb_all[i], g_in)
        for d in back + (0,):
            j = lax.rem(y + d, ny)
            sg_send[j, 0] = mm(s_row, pre[j, sl:]) + pre[j, :sl]
            sg_send[j, 1] = mm(g_in, suf[j, sl:]) + suf[j, :sl]
            if d:
                sg_copy(d).start()
        sg_all[slot] = sg_send[y]

    for n in range(HOLD):

        @pl.when(jnp.logical_or(slot != n, jnp.logical_not(holds)))
        def _():
            remote(sg_all.at[n], sg_all.at[n], a2_ss.at[0], a2_rs.at[n], partner).wait_recv()

    st = sg_all[:, 0].reshape(DK, DK)
    gt = sg_all[:, 1].reshape(DK, DK)

    u, w, att_do, k_end, inv_t, ratio, ratio_t = (sv[n] for n in range(7))
    fresh = u - mm_nt(w, st)
    d_fresh = att_do + mm_nt(k_end, gt)
    do = do_ref[...].astype(f32)
    d_qg = mm(do, st)
    dx = mm(inv_t, d_fresh)
    d_ke = mm(fresh, gt)
    d_att = jnp.where(lower, mm_nt(do, fresh), 0.0)
    d_att_t = jnp.where(upper, mm_nt(fresh, do), 0.0)
    dy = -mm(dx, st)
    d_lo = jnp.where(row > col, -mm_nt(dx, fresh), 0.0)
    d_lo_t = jnp.where(row < col, -mm_nt(fresh, dx), 0.0)
    bare, lo, att, att_t, k, qn, y_in, lo_t = (sv[n] for n in range(7, 15))
    beta, grown, rest, k_scale, q_scale, sig = (cols[n] for n in range(6))
    q = qn * (DK ** (-0.5))
    v = proj_ref[2].astype(f32)
    sym = d_lo * ratio * beta + d_lo_t * ratio_t * beta_row
    dq = mm(d_att * ratio, k) + grown * d_qg
    dk = mm(d_att_t * ratio_t, q) + mm(sym, k) + (beta * grown) * dy + rest * d_ke
    ke_part = d_ke * k_end
    d_beta = row_sum(d_lo * bare + dx * v + grown * dy * k)
    mixed = d_lo * lo - d_lo_t * lo_t + d_att * att - d_att_t * att_t
    mixed = mixed + dy * y_in + d_qg * (grown * q) - ke_part
    dg_row = to_row(row_sum(mixed))
    tail = col_sum(row_sum(ke_part + last * (st * gt)))
    d_decay = row_sum(jnp.where(col >= row, dg_row, 0.0)) + tail
    d_l0 = -rate * sig * d_decay
    d_l1 = d_beta * beta * (1.0 - beta)
    dq = (q_scale * (DK ** (-0.5))) * (dq - qn * row_sum(dq * qn))
    dk = k_scale * (dk - k * row_sum(dk * k))
    dqk = jnp.concatenate([dq.astype(bf16), dk.astype(bf16)], 1)
    dv = (beta * dx).astype(bf16)

    loads[4].wait()
    loads[5].wait()
    wide_l0 = jnp.concatenate([d_l0, d_l0], 1)
    wide_l1 = jnp.concatenate([d_l1, d_l1], 1)

    def compute(d):
        at = pl.multiple_of(lax.rem(z + d + nz, nz) * (2 * DK), 2 * DK)
        here = pl.ds(at, 2 * DK)
        both = jnp.concatenate([wv[0, here, :], wv[1, here, :]], 1)
        out = dot(dqk, both, 1) + dot(dv, wv[2, here, :], 1)
        gates = gate_ref[:, here].astype(f32)
        out = out + wide_l0 * gates[0:1] + wide_l1 * gates[1:2]
        term[d % nz, 0] = out[:, :DK]
        term[d % nz, 1] = out[:, DK:]
        pair(d).start()

    def pair(d):
        d = d % nz
        return remote(term.at[d, 1 - c], pair_recv.at[d], p_ss.at[d], p_rs.at[d], partner)

    def summed(d):
        pair(d).wait_recv()
        return term[d % nz, c] + pair_recv[d % nz]

    part = DK // 2
    msgs = {
        ("far", 1): (0, pl.ds(0, part), 2),
        ("far", -1): (0, pl.ds(part, part), -2),
        ("mid", 1): (1, pl.ds(0, DK), 1),
        ("mid", -1): (2, pl.ds(0, DK), -1),
        ("two", 1): (3, pl.ds(0, DK), 2),
        ("two", -1): (4, pl.ds(0, DK), -2),
        ("one", 1): (5, pl.ds(0, DK), 1),
        ("one", -1): (6, pl.ds(0, DK), -1),
    }

    def msg(name):
        at, rows, d = msgs[name]
        n = list(msgs).index(name)
        return remote(
            z_send.at[at, rows], z_recv.at[at, rows], z_ss.at[n], z_rs.at[n], z_peer(d)
        )

    for d in (4, 3, -3):
        compute(d)
    compute(1)
    z_send[0] = summed(4)
    msg(("far", 1)).start()
    msg(("far", -1)).start()
    compute(-1)
    for sign in (1, -1):
        z_send[msgs["mid", sign][0]] = summed(3 * sign)
        msg(("mid", sign)).start()
    compute(2)
    compute(-2)
    compute(0)
    for sign in (1, -1):
        z_send[msgs["one", sign][0]] = summed(sign)
        msg(("one", sign)).start()
    two = {sign: summed(2 * sign) for sign in (1, -1)}
    total = summed(0)
    for sign in (1, -1):
        at = msgs["two", sign][0]
        msg(("far", sign)).wait_recv()
        msg(("mid", sign)).wait_recv()
        value = two[sign] + z_recv[msgs["mid", sign][0]]
        rows = msgs["far", sign][1]
        z_send[at] = value
        z_send[at, rows] = z_send[at, rows] + z_recv[0, rows]
        msg(("two", sign)).start()
    for sign in (1, -1):
        msg(("one", sign)).wait_recv()
        total = total + z_recv[msgs["one", sign][0]]
    for sign in (1, -1):
        msg(("two", sign)).wait_recv()
        total = total + z_recv[msgs["two", sign][0]]
    out_ref[...] = total.astype(bf16)

    to_holders(lambda n, dev: m_copy(n, dev).wait_send())
    to_holders(lambda n, dev: bf_copy(n, dev).wait_send())

    @pl.when(holds)
    def _():
        for d in range(1, nx):
            xb_copy(d).wait_send()

        @pl.when(in_middle)
        def _():
            for d in range(1, nx):
                xm_copy(d).wait_send()

        for d in range(1, ny):
            sg_copy(d).wait_send()

    for d in range(nz):
        pair(d).wait_send()
    for name in msgs:
        msg(name).wait_send()


def shards(nx, nz, projected, out_grad, logits, head_params, qkv_weight, gate_weight):
    head_params = head_params.T
    gate_weight = gate_weight.transpose(1, 0, 2).reshape(gate_weight.shape[0], -1)
    sl, ny = DK // HOLD, ROW
    dma = pltpu.SemaphoreType.DMA
    scratch = [
        pltpu.VMEM(projected.shape, bf16),
        pltpu.VMEM(out_grad.shape, bf16),
        pltpu.VMEM(logits.shape, f32),
        pltpu.VMEM(head_params.shape, f32),
        pltpu.VMEM(gate_weight.shape, bf16),
        pltpu.VMEM(qkv_weight.shape, bf16),
        pltpu.VMEM((15, DK, DK), f32),
        pltpu.VMEM((6, DK, DK), f32),
        pltpu.VMEM((ny, DK, DK), f32),
        pltpu.VMEM((HOLD, 2, sl, DK), f32),
        pltpu.VMEM((ny, 2, sl, DK), f32),
        pltpu.VMEM((ny, sl + DK, DK), f32),
        pltpu.VMEM((ny, sl + DK, DK), f32),
        pltpu.VMEM((nx, DK, DK), f32),
        pltpu.VMEM((2, sl, DK), f32),
        pltpu.VMEM((nx, sl, DK), f32),
        pltpu.VMEM((ny, 2, sl, DK), f32),
        pltpu.VMEM((HOLD, 2, sl, DK), f32),
        pltpu.VMEM((nz, 2, DK, DK), f32),
        pltpu.VMEM((nz, DK, DK), f32),
        pltpu.VMEM((7, DK, DK), f32),
        pltpu.VMEM((7, DK, DK), f32),
        dma((6,)),
        dma((HOLD,)),
        dma((ny,)),
        dma((HOLD,)),
        dma((ny,)),
        dma((nx - 1,)),
        dma((nx,)),
        dma((nx - 1,)),
        dma((nx,)),
        dma((ny,)),
        dma((HOLD,)),
        dma((nz,)),
        dma((nz,)),
        dma((8,)),
        dma((8,)),
    ]
    return pl.pallas_call(
        functools.partial(kernel, nx, nz),
        out_shape=jax.ShapeDtypeStruct((DK, DK), bf16),
        in_specs=[pl.BlockSpec(memory_space=pltpu.HBM)] * 6,
        out_specs=pl.BlockSpec(memory_space=pltpu.VMEM),
        scratch_shapes=scratch,
        compiler_params=pltpu.CompilerParams(
            collective_id=0, has_side_effects=True, vmem_limit_bytes=67043328
        ),
        name="delta_backward",
    )(projected, out_grad, logits, head_params, qkv_weight, gate_weight)


def solution(mesh):
    nx, nz = mesh.shape["seq"] // ROW, mesh.shape["head"] // 2
    in_specs = (
        P(None, "seq", "head"),
        P("seq", "head"),
        P(None, "head", "seq"),
        P(None, "head"),
        P(None, None, "head"),
        P(None, "head", None),
    )
    return jax.shard_map(
        functools.partial(shards, nx, nz),
        mesh=mesh,
        in_specs=in_specs,
        out_specs=P("seq", "head"),
        check_vma=False,
    )
```

time: 71 us -> 51.8 us (0.73)
  the two profiles are of different devices: /device:TPU:64 before, /device:TPU:1 now
where the time goes in v2:
time: 51.8 us; the launch traced here: 51.7 us
  Pallas kernels  50.3 us (97%)
  local copies, waits for them, and re-layouts  1.38 us (3%)
    pallas_call x1, Pallas kernels, shards(): pl.pallas_call(functools.partial(kernel, nx, nz), out_shape=jax.ShapeDtyp...  50.3 us
    unnamed x1, local copies, waits for them, and re-layouts  1.38 us

profile of v2, /device:TPU:1, one launch (start us, length us, event | category | flops | bytes accessed | tf_op | source)
XLA Modules:
  0.0 51.7 jit_solution(7961719051368466501)
XLA Ops:
  0.0 50.3 %delta_backward.1 = bf16[128,128]{1,0:T(8,128)(2,1)} custom-call(bf16[3,128,128]{2,1,0:T(8,128)(2,1)} %proj_hbm.1, bf16[128,128]{1,0:T(8,128)(2,1)} %do_hbm.1, f32[2,1,128]{2,1,0:T(1,128)} %logit_hbm.1, f32[1,2]{1,0:T(1,128)} %bitcast.3, bf16[3,2048,128]{2,1,0:T(8,128)(2,1)} %w_hbm.1, bf16[2,2048]{1,0:T(2,128)(2,1)} %bitcast.2), custom_call_target="tpu_custom_call" | custom-call | tf_op jit(solution)/shard_map/delta_backward/pallas_call | solution.py:527
  50.3 1.4 %copy.8 = bf16[128,128]{1,0:T(8,128)(2,1)} copy(bf16[128,128]{1,0:T(8,128)(2,1)} %delta_backward.1) | data formatting | bytes 65536

commit v3 on v2

--- a/solution.py
+++ b/solution.py
@@ -294,26 +294,39 @@
     @pl.when(holds)
     def _():
         from_row(m_all, ag_ss, ag_rs)
-        from_row(bf_all, a1_ss, a1_rs)
-        zeros = jnp.zeros((sl, DK), f32)
-        pad = jnp.zeros((DK, DK), f32)
-        fwd = bwd = jnp.concatenate([zeros, jnp.where(eye, 1.0, 0.0)], 0)
+        fwd = bwd = jnp.where(eye, 1.0, 0.0)
         for n in range(ny):
             j, i = n, ny - 1 - n
-            pre[j] = fwd
-            suf[i] = bwd
-            fwd = mm_nt(fwd, m_all[j]) + jnp.concatenate([bf_all[j, 0], pad], 0)
-            bwd = mm(bwd, m_all[i]) + jnp.concatenate([bf_all[i, 1], pad], 0)
-        xm_all[x] = bwd[sl:]
-        xb_own[0] = fwd[:sl]
-        xb_own[1] = bwd[:sl]
-        for d in (2, 1, 3) if nx == 4 else range(1, nx):
-            xb_copy(d).start()
+            pre[j, sl:] = fwd
+            suf[i, sl:] = bwd
+            fwd = mm_nt(fwd, m_all[j]) if n else m_all[j].T
+            bwd = mm(bwd, m_all[i]) if n else m_all[i]
+        xm_all[x] = bwd
 
         @pl.when(in_middle)
         def _():
             for d in (2, 1, 3) if nx == 4 else range(1, nx):
                 xm_copy(d).start()
+
+        from_row(bf_all, a1_ss, a1_rs)
+        b_sum, f_sum = bf_all[ny - 1, 0], bf_all[0, 1]
+        for n in range(1, ny):
+            b_sum = b_sum + mm_nt(bf_all[n - 1, 0], suf[n - 1, sl:])
+            f_sum = f_sum + mm_nt(bf_all[n, 1], pre[n, sl:])
+        xb_own[0] = b_sum
+        xb_own[1] = f_sum
+        for d in (2, 1, 3) if nx == 4 else range(1, nx):
+            xb_copy(d).start()
+
+        zeros = jnp.zeros((sl, DK), f32)
+        fwd = bwd = zeros
+        for n in range(ny):
+            j, i = n, ny - 1 - n
+            pre[j, :sl] = fwd
+            suf[i, :sl] = bwd
+            if n < ny - 1:
+                fwd = (mm_nt(fwd, m_all[j]) if n else 0.0) + bf_all[j, 0]
+                bwd = (mm(bwd, m_all[i]) if n else 0.0) + bf_all[i, 1]
 
         xb_all[x] = zeros
         for n in range(nx):
@@ -521,20 +534,20 @@
         dma((HOLD,)),
         dma((nz,)),
         dma((nz,)),
-        dma((8,)),
-        dma((8,)),
+        dma((12,)),
+        dma((12,)),
     ]
     return pl.pallas_call(
         functools.partial(kernel, nx, nz),
-        out_shape=jax.ShapeDtypeStruct((DK, DK), bf16),
+        out_shape=pltpu.VMEM((DK, DK), bf16),
         in_specs=[pl.BlockSpec(memory_space=pltpu.HBM)] * 6,
         out_specs=pl.BlockSpec(memory_space=pltpu.VMEM),
         scratch_shapes=scratch,
         compiler_params=pltpu.CompilerParams(
-            collective_id=0, has_side_effects=True, vmem_limit_bytes=67043328
+            collective_id=0, has_side_effects=True, vmem_limit_bytes=48000000
         ),
         name="delta_backward",
-    )(projected, out_grad, logits, head_params, qkv_weight, gate_weight)
+    )(*(pltpu.with_memory_space_constraint(a, pltpu.HBM) for a in (projected, out_grad, logits, head_params, qkv_weight, gate_weight)))
 
 
 def solution(mesh):

time: 51.8 us -> 49 us (0.946)
  Pallas kernels: 50.3 us -> 48.2 us
  local copies, waits for them, and re-layouts: 1.38 us -> 0.62 us
    pallas_call x1, Pallas kernels: 50.3 us -> 48.2 us  [shards(): pl.pallas_call(functools.partial(kernel, nx, nz), out_shape=pltpu.VMEM((D...]
    unnamed x1, local copies, waits for them, and re-layouts: 1.38 us -> 0.62 us
where the time goes in v3:
time: 49 us; the launch traced here: 48.9 us
  Pallas kernels  48.2 us (98%)
  local copies, waits for them, and re-layouts  0.62 us (1%)
    pallas_call x1, Pallas kernels, shards(): pl.pallas_call(functools.partial(kernel, nx, nz), out_shape=pltpu.VMEM((D...  48.2 us

profile of v3, /device:TPU:1, one launch (start us, length us, event | category | flops | bytes accessed | tf_op | source)
XLA Modules:
  0.0 48.9 jit_solution(1449816448825934905)
XLA Ops:
  0.0 48.2 %delta_backward.1 = bf16[128,128]{1,0:T(8,128)(2,1)S(1)} custom-call(bf16[3,128,128]{2,1,0:T(8,128)(2,1)} %proj_hbm.1, bf16[128,128]{1,0:T(8,128)(2,1)} %do_hbm.1, f32[2,1,128]{2,1,0:T(1,128)} %logit_hbm.1, f32[1,2]{1,0:T(1,128)} %bitcast.3, bf16[3,2048,128]{2,1,0:T(8,128)(2,1)} %w_hbm.1, bf16[2,2048]{1,0:T(2,128)(2,1)} %bitcast.2), custom_call_target="tpu_custom_call" | custom-call | tf_op jit(solution)/shard_map/delta_backward/pallas_call | solution.py:540
  48.2 0.6 %copy.8 = bf16[128,128]{1,0:T(8,128)(2,1)} copy(bf16[128,128]{1,0:T(8,128)(2,1)S(1)} %delta_backward.1) | data formatting | bytes 65536

commit v4 on v3

--- a/solution.py
+++ b/solution.py
@@ -268,7 +268,9 @@
     to_holders(lambda n, dev: bf_copy(n, dev).start())
     bf_all[y] = bf_own[slot]
     att_t = ratio_t * mm_nt(k, q)
-    saved = (u, w, mm(att_t, do), k_end, inv.T, ratio, ratio_t, bare, lo, att, att_t, k, qn, y_in)
+    inv_t = inv.T
+    dx_free, dx_state = mm(inv_t, mm(att_t, do)), mm(inv_t, k_end)
+    saved = (u, w, dx_free, k_end, dx_state, ratio, ratio_t, bare, lo, att, att_t, k, qn, y_in)
     for n, value in enumerate(saved):
         sv[n] = value
     sv[len(saved)] = jnp.where(row < col, ratio_t * inner * beta_row, 0.0)
@@ -360,12 +362,11 @@
     st = sg_all[:, 0].reshape(DK, DK)
     gt = sg_all[:, 1].reshape(DK, DK)
 
-    u, w, att_do, k_end, inv_t, ratio, ratio_t = (sv[n] for n in range(7))
+    u, w, dx_free, k_end, dx_state, ratio, ratio_t = (sv[n] for n in range(7))
     fresh = u - mm_nt(w, st)
-    d_fresh = att_do + mm_nt(k_end, gt)
     do = do_ref[...].astype(f32)
     d_qg = mm(do, st)
-    dx = mm(inv_t, d_fresh)
+    dx = dx_free + mm_nt(dx_state, gt)
     d_ke = mm(fresh, gt)
     d_att = jnp.where(lower, mm_nt(do, fresh), 0.0)
     d_att_t = jnp.where(upper, mm_nt(fresh, do), 0.0)

time: 49 us -> 48.9 us (level)
  no operation moved by 1% of the time
where the time goes in v4:
time: 48.9 us; the launch traced here: 48.8 us
  Pallas kernels  48.2 us (99%)
  local copies, waits for them, and re-layouts  0.62 us (1%)
    pallas_call x1, Pallas kernels, shards(): pl.pallas_call(functools.partial(kernel, nx, nz), out_shape=pltpu.VMEM((D...  48.2 us

profile of v4, /device:TPU:1, one launch (start us, length us, event | category | flops | bytes accessed | tf_op | source)
XLA Modules:
  0.0 48.8 jit_solution(12917266029707601373)
XLA Ops:
  0.0 48.2 %delta_backward.1 = bf16[128,128]{1,0:T(8,128)(2,1)S(1)} custom-call(bf16[3,128,128]{2,1,0:T(8,128)(2,1)} %proj_hbm.1, bf16[128,128]{1,0:T(8,128)(2,1)} %do_hbm.1, f32[2,1,128]{2,1,0:T(1,128)} %logit_hbm.1, f32[1,2]{1,0:T(1,128)} %bitcast.3, bf16[3,2048,128]{2,1,0:T(8,128)(2,1)} %w_hbm.1, bf16[2,2048]{1,0:T(2,128)(2,1)} %bitcast.2), custom_call_target="tpu_custom_call" | custom-call | tf_op jit(solution)/shard_map/delta_backward/pallas_call | solution.py:541
  48.2 0.6 %copy.8 = bf16[128,128]{1,0:T(8,128)(2,1)} copy(bf16[128,128]{1,0:T(8,128)(2,1)S(1)} %delta_backward.1) | data formatting | bytes 65536

commit v5 on v4

--- a/solution.py
+++ b/solution.py
@@ -331,20 +331,24 @@
                 bwd = (mm(bwd, m_all[i]) if n else 0.0) + bf_all[i, 1]
 
         xb_all[x] = zeros
-        for n in range(nx):
-
-            @pl.when(x != n)
-            def _():
-                if n in middle:
-                    remote(xm_all.at[n], xm_all.at[n], xm_ss.at[0], xm_rs.at[n], partner).wait_recv()
-                remote(xb_all.at[n], xb_all.at[n], xb_ss.at[0], xb_rs.at[n], partner).wait_recv()
-
-        s_row = jnp.where(x > 0, xb_all[0], 0.0)
-        g_in = jnp.where(x < nx - 1, xb_all[nx - 1], 0.0)
-        for n in middle:
-            i = nx - 1 - n
-            s_row = jnp.where(x > n, mm_nt(s_row, xm_all[n]) + xb_all[n], s_row)
-            g_in = jnp.where(x < i, mm(g_in, xm_all[i]) + xb_all[i], g_in)
+
+        def from_rows(ref, rs, rows):
+            for n in rows:
+
+                @pl.when(x != n)
+                def _():
+                    remote(ref.at[n], ref.at[n], xb_ss.at[0], rs.at[n], partner).wait_recv()
+
+        from_rows(xm_all, xm_rs, middle)
+        both = mm(xm_all[2], xm_all[1])
+        from_rows(xb_all, xb_rs, range(nx))
+        v = [xb_all[n] for n in range(nx)]
+        s_two = mm_nt(v[0], xm_all[1]) + v[1]
+        s_three = mm_nt(v[0], both) + mm_nt(v[1], xm_all[2]) + v[2]
+        s_row = jnp.where(x > 2, s_three, jnp.where(x > 1, s_two, jnp.where(x > 0, v[0], 0.0)))
+        g_one = mm(v[3], xm_all[2]) + v[2]
+        g_none = mm(v[3], both) + mm(v[2], xm_all[1]) + v[1]
+        g_in = jnp.where(x < 1, g_none, jnp.where(x < 2, g_one, jnp.where(x < 3, v[3], 0.0)))
         for d in back + (0,):
             j = lax.rem(y + d, ny)
             sg_send[j, 0] = mm(s_row, pre[j, sl:]) + pre[j, :sl]

time: 48.9 us -> 48.9 us (level)
  no operation moved by 1% of the time
where the time goes in v5:
time: 48.9 us; the launch traced here: 48.8 us
  Pallas kernels  48.2 us (99%)
  local copies, waits for them, and re-layouts  0.62 us (1%)
    pallas_call x1, Pallas kernels, shards(): pl.pallas_call(functools.partial(kernel, nx, nz), out_shape=pltpu.VMEM((D...  48.2 us

profile of v5, /device:TPU:1, one launch (start us, length us, event | category | flops | bytes accessed | tf_op | source)
XLA Modules:
  0.0 48.8 jit_solution(1785482804012333133)
XLA Ops:
  0.0 48.2 %delta_backward.1 = bf16[128,128]{1,0:T(8,128)(2,1)S(1)} custom-call(bf16[3,128,128]{2,1,0:T(8,128)(2,1)} %proj_hbm.1, bf16[128,128]{1,0:T(8,128)(2,1)} %do_hbm.1, f32[2,1,128]{2,1,0:T(1,128)} %logit_hbm.1, f32[1,2]{1,0:T(1,128)} %bitcast.3, bf16[3,2048,128]{2,1,0:T(8,128)(2,1)} %w_hbm.1, bf16[2,2048]{1,0:T(2,128)(2,1)} %bitcast.2), custom_call_target="tpu_custom_call" | custom-call | tf_op jit(solution)/shard_map/delta_backward/pallas_call | solution.py:545
  48.2 0.6 %copy.8 = bf16[128,128]{1,0:T(8,128)(2,1)} copy(bf16[128,128]{1,0:T(8,128)(2,1)S(1)} %delta_backward.1) | data formatting | bytes 65536
